TPU v7x, 128 devices: a whole 4x4x4 slice. The times are simulated.
128 devices in a mesh: ctx: 4 (over y), heads: 32 (over x, z, core).
Axes of the slice: x: 4, y: 4, z: 4, core: 2. Of those that a mesh axis runs over, the one named last changes fastest.
Arguments:
- queries: float32 [32768, 4096], P(('ctx', 'heads')), may hold values from -110 to 110
- keys: float32 [32768, 4096], P(('ctx', 'heads')), may hold values from -4 to 4
- values: float32 [32768, 4096], P(('ctx', 'heads')), may hold values from -12 to 12
- merge_keys: float32 [6, 256, 512], replicated, may hold values from -0.25 to 0.25
- merge_values: float32 [6, 256, 512], replicated, may hold values from -0.25 to 0.25
- out_gain: float32 [32, 128], P('heads'), may hold values from 0.1 to 1.9
Outputs:
- attended: float32 [32768, 4096], P(('ctx', 'heads'))
All inputs are finite; a program needn't handle non-finite values.
Results may differ from a plain program's by a relative error of at most 0.0003.
Values sent between devices are 32-bit elements; how exact they have to be, the bound alone decides.
A program may use at most 256 MiB of HBM per device.

v0:
```python
import math

import jax
import jax.numpy as jnp
from jax import lax
from jax.sharding import PartitionSpec as P


def from_partner(block, axis, distance):
    count = lax.axis_size(axis)
    route = []
    for low in range(count):
        high = low | 1 << distance
        if high != low and high < count:
            route += [(low, high), (high, low)]
    return lax.ppermute(block, axis, route)


def merge_nodes(matrix, children):
    node_count = children.shape[0] // 2
    paired = children.reshape(node_count, 2 * children.shape[1], children.shape[2])
    return jnp.einsum("ij,njw->niw", matrix, paired, precision=lax.Precision.HIGHEST)


def sibling_nodes(key_nodes):
    node_count, row_count, feature_width = key_nodes.shape
    return key_nodes.reshape(node_count // 2, 2, row_count, feature_width)[:, ::-1].reshape(
        node_count, row_count, feature_width
    )


def local_levels(key_rows, value_rows, merge_keys, merge_values):
    leaf_rows = merge_keys.shape[1]
    feature_width = key_rows.shape[1]
    key_nodes = key_rows.reshape(-1, leaf_rows, feature_width)
    value_nodes = value_rows.reshape(-1, leaf_rows, feature_width)
    tree_depth = key_nodes.shape[0].bit_length() - 1
    groups = [(key_nodes, value_nodes)]
    for level_index in range(tree_depth):
        groups.append((sibling_nodes(key_nodes), sibling_nodes(value_nodes)))
        key_nodes = merge_nodes(merge_keys[level_index], key_nodes)
        value_nodes = merge_nodes(merge_values[level_index], value_nodes)
    return (groups, key_nodes[0], value_nodes[0], tree_depth)


def swap_levels(top_key, top_value, merge_keys, merge_values, tree_depth):
    bit_count = lax.axis_size("ctx").bit_length() - 1
    ctx_place = lax.axis_index("ctx")
    groups = []
    for bit_index in range(bit_count):
        other_key, other_value = from_partner((top_key, top_value), "ctx", bit_index)
        groups.append((other_key[None], other_value[None]))
        if bit_index + 1 < bit_count:
            is_upper = ctx_place // 2**bit_index % 2 == 1
            lower_key = jnp.where(is_upper, other_key, top_key)
            higher_key = jnp.where(is_upper, top_key, other_key)
            lower_value = jnp.where(is_upper, other_value, top_value)
            higher_value = jnp.where(is_upper, top_value, other_value)
            top_key = merge_nodes(
                merge_keys[tree_depth + bit_index], jnp.stack([lower_key, higher_key])
            )[0]
            top_value = merge_nodes(
                merge_values[tree_depth + bit_index], jnp.stack([lower_value, higher_value])
            )[0]
    return groups


def summary_groups(key_rows, value_rows, merge_keys, merge_values):
    groups, top_key, top_value, tree_depth = local_levels(
        key_rows, value_rows, merge_keys, merge_values
    )
    groups = groups + swap_levels(top_key, top_value, merge_keys, merge_values, tree_depth)
    return groups


def absorb(carry_state, query_rows, key_group, value_group, head_count, score_scale):
    biggest, weight_sum, accumulated = carry_state
    node_count, row_count, feature_width = key_group.shape
    query_count = query_rows.shape[0]
    head_size = feature_width // head_count
    per_node = query_count // node_count
    grouped = query_rows.reshape(node_count, per_node, head_count, head_size)
    key_split = key_group.reshape(node_count, row_count, head_count, head_size)
    value_split = value_group.reshape(node_count, row_count, head_count, head_size)
    scores = (
        jnp.einsum("nqhd,nkhd->nqhk", grouped, key_split, precision=lax.Precision.HIGHEST)
        * score_scale
    )
    scores = scores.reshape(query_count, head_count, row_count)
    running_max = jnp.maximum(biggest, jnp.max(scores, axis=-1))
    weights = jnp.exp(scores - running_max[..., None])
    factor = jnp.exp(biggest - running_max)
    weight_sum = weight_sum * factor + jnp.sum(weights, axis=-1)
    added_values = jnp.einsum(
        "nqhk,nkhd->nqhd",
        weights.reshape(node_count, per_node, head_count, row_count),
        value_split,
        precision=lax.Precision.HIGHEST,
    )
    accumulated = accumulated * factor[..., None] + added_values.reshape(
        query_count, head_count, head_size
    )
    return (running_max, weight_sum, accumulated)


def shards(queries, keys, values, merge_keys, merge_values, out_gain):
    head_count = out_gain.shape[0]
    head_size = out_gain.shape[1]
    score_scale = 1.0 / math.sqrt(head_size)
    query_rows, key_rows, value_rows = (
        lax.all_to_all(queries, "heads", split_axis=1, concat_axis=0, tiled=True),
        lax.all_to_all(keys, "heads", split_axis=1, concat_axis=0, tiled=True),
        lax.all_to_all(values, "heads", split_axis=1, concat_axis=0, tiled=True),
    )
    groups = summary_groups(key_rows, value_rows, merge_keys, merge_values)
    query_count = query_rows.shape[0]
    carry_state = (
        jnp.full((query_count, head_count), -jnp.inf, jnp.float32),
        jnp.zeros((query_count, head_count), jnp.float32),
        jnp.zeros((query_count, head_count, head_size), jnp.float32),
    )
    for key_group, value_group in groups:
        carry_state = absorb(
            carry_state, query_rows, key_group, value_group, head_count, score_scale
        )
    context = carry_state[2] / carry_state[1][..., None]
    mean_square = jnp.mean(context * context, axis=-1, keepdims=True)
    normed = context * lax.rsqrt(mean_square + 1e-06) * out_gain
    return lax.all_to_all(
        normed.reshape(query_count, head_count * head_size),
        "heads",
        split_axis=0,
        concat_axis=1,
        tiled=True,
    )


def solution(mesh):
    return jax.shard_map(
        shards,
        mesh=mesh,
        in_specs=(
            P(("ctx", "heads"), None),
            P(("ctx", "heads"), None),
            P(("ctx", "heads"), None),
            P(),
            P(),
            P("heads", None),
        ),
        out_specs=P(("ctx", "heads"), None),
        check_vma=False,
    )
```

profile of v0, /device:TPU:1, one launch (start us, length us, event | category | flops | bytes accessed | tf_op | source)
XLA Modules:
  0.0 607.0 jit_solution(16235530136003453755)
XLA Ops:
  11.2 9.5 %all-to-all-start = ((f32[256,32,128]{2,0,1:T(8,128)}), f32[256,32,128]{2,0,1:T(8,128)}, u32[]{:S(2)}, u32[]{:S(2)}) async-start(f32[256,32,128]{2,0,1:T(8,128)} %copy.28), calls=%async_computation | async-start | bytes 8388608 | tf_op jit(solution)/shard_map/all_to_all | solution.py:112
  31.8 40.9 %all-to-all-done = f32[256,32,128]{2,0,1:T(8,128)} async-done(((f32[256,32,128]{2,0,1:T(8,128)}), f32[256,32,128]{2,0,1:T(8,128)}, u32[]{:S(2)}, u32[]{:S(2)}) %all-to-all-start) | async-done | bytes 4194336 | tf_op jit(solution)/shard_map/all_to_all | solution.py:112
  72.8 7.1 %all-to-all-start.1 = ((f32[256,32,128]{2,0,1:T(8,128)}), f32[256,32,128]{2,0,1:T(8,128)}, u32[]{:S(2)}, u32[]{:S(2)}) async-start(f32[256,32,128]{2,0,1:T(8,128)} %copy.30), calls=%async_computation.1 | async-start | bytes 8388608 | tf_op jit(solution)/shard_map/all_to_all | solution.py:111
  85.5 5.6 copy.32
  91.1 8.6 %fusion.94 = f32[16,128,256]{2,1,0:T(8,128)S(1)} fusion(f32[16,512,128]{2,1,0:T(8,128)} %bitcast.18, f32[6,256,512]{2,1,0:T(8,128)} %param.9), kind=kOutput, calls=%fused_computation.105 | convolution fusion | flops 3221225472 | bytes 6815744 | tf_op jit(solution)/shard_map/ij,njw->niw/dot_general | solution.py:22
  101.5 30.5 %all-to-all-done.1 = f32[256,32,128]{2,0,1:T(8,128)} async-done(((f32[256,32,128]{2,0,1:T(8,128)}), f32[256,32,128]{2,0,1:T(8,128)}, u32[]{:S(2)}, u32[]{:S(2)}) %all-to-all-start.1) | async-done | bytes 4194336 | tf_op jit(solution)/shard_map/all_to_all | solution.py:111
  132.0 7.5 %all-to-all-start.2 = ((f32[256,32,128]{2,0,1:T(8,128)}), f32[256,32,128]{2,0,1:T(8,128)}, u32[]{:S(2)}, u32[]{:S(2)}) async-start(f32[256,32,128]{2,0,1:T(8,128)} %copy.32), calls=%async_computation.2 | async-start | bytes 8388608 | tf_op jit(solution)/shard_map/all_to_all | solution.py:113
  157.5 11.3 %bitcast_reduce_fusion.1 = (f32[4,2048]{1,0:T(4,128)S(1)}, f32[4,256,2048]{2,1,0:T(8,128)}) fusion(f32[4,256,128]{1,2,0:T(8,128)} %bitcast.506, f32[4,2048,128]{2,1,0:T(8,128)} %bitcast.64), kind=kOutput, calls=%fused_computation.24 | convolution fusion | flops 3225411584 | bytes 13139968 | tf_op jit(solution)/shard_map/nqhd,nkhd->nqhk/dot_general | solution.py:86
  170.6 11.7 %bitcast_reduce_fusion.2 = (f32[8,1024]{1,0:T(8,128)S(1)}, f32[8,256,1024]{2,1,0:T(8,128)}) fusion(f32[8,256,128]{1,2,0:T(8,128)} %bitcast.504, f32[8,1024,128]{2,1,0:T(8,128)} %bitcast.44), kind=kOutput, calls=%fused_computation.29 | convolution fusion | flops 3225411584 | bytes 13664256 | tf_op jit(solution)/shard_map/nqhd,nkhd->nqhk/dot_general | solution.py:86
  184.5 12.5 %bitcast_reduce_fusion.3 = (f32[16,512]{1,0:T(8,128)S(1)}, f32[16,256,512]{2,1,0:T(8,128)}) fusion(f32[16,256,128]{1,2,0:T(8,128)} %bitcast.494, f32[16,512,128]{2,1,0:T(8,128)} %bitcast.24), kind=kOutput, calls=%fused_computation.34 | convolution fusion | flops 3225411584 | bytes 14712832 | tf_op jit(solution)/shard_map/nqhd,nkhd->nqhk/dot_general | solution.py:86
  202.3 13.7 %bitcast_reduce_fusion.5 = (f32[32,256]{1,0:T(8,128)S(1)}, f32[32,256,256]{2,1,0:T(8,128)}) fusion(f32[256,32,128]{2,0,1:T(8,128)} %all-to-all-done.1, f32[256,32,128]{2,0,1:T(8,128)} %all-to-all-done), kind=kOutput, calls=%fused_computation.44 | convolution fusion | flops 3225411584 | bytes 16809984 | tf_op jit(solution)/shard_map/nqhd,nkhd->nqhk/dot_general | solution.py:86
  216.0 11.1 %bitcast_reduce_fusion.4 = (f32[32,256]{1,0:T(8,128)S(1)}, f32[32,256,256]{2,1,0:T(8,128)}) fusion(f32[32,256,128]{2,1,0:T(8,128)S(1)} %bitcast.487, f32[256,32,128]{2,0,1:T(8,128)} %all-to-all-done.1), kind=kOutput, calls=%fused_computation.39 | convolution fusion | flops 3225411584 | bytes 16809984 | tf_op jit(solution)/shard_map/nqhd,nkhd->nqhk/dot_general | solution.py:86
  232.7 8.6 %fusion.92 = f32[16,128,256]{2,1,0:T(8,128)S(1)} fusion(f32[16,512,128]{2,1,0:T(8,128)} %bitcast.27, f32[6,256,512]{2,1,0:T(8,128)} %param.10), kind=kOutput, calls=%fused_computation.103 | convolution fusion | flops 3221225472 | bytes 6815744 | tf_op jit(solution)/shard_map/ij,njw->niw/dot_general | solution.py:22
  275.6 11.3 %fusion.69 = f32[4,2048,1,128]{1,3,0,2:T(8,128)} fusion(f32[4,256,128]{1,2,0:T(8,128)S(1)} %bitcast.505, f32[4,256,2048]{2,1,0:T(8,128)} %get-tuple-element.41, f32[4,2048]{1,0:T(4,128)S(1)} %maximum_maximum_fusion.1), kind=kOutput, calls=%fused_computation.80 | convolution fusion | flops 3225419776 | bytes 13139968 | tf_op jit(solution)/shard_map/nqhk,nkhd->nqhd/dot_general | solution.py:94
  293.7 11.4 %fusion.75 = f32[8,1024,1,128]{1,3,0,2:T(8,128)} fusion(f32[8,256,128]{1,2,0:T(8,128)S(1)} %bitcast.503, f32[8,256,1024]{2,1,0:T(8,128)} %get-tuple-element.43, f32[8,1024]{1,0:T(8,128)S(1)} %maximum_maximum_fusion.2), kind=kOutput, calls=%fused_computation.82 | convolution fusion | flops 3225419776 | bytes 13664256 | tf_op jit(solution)/shard_map/nqhk,nkhd->nqhd/dot_general | solution.py:94
  311.6 11.5 %fusion.72 = f32[16,512,1,128]{1,3,0,2:T(8,128)} fusion(f32[16,256,128]{1,2,0:T(8,128)S(1)} %bitcast.493, f32[16,256,512]{2,1,0:T(8,128)} %get-tuple-element.45, f32[16,512]{1,0:T(8,128)S(1)} %copy-done.10), kind=kOutput, calls=%fused_computation.81 | convolution fusion | flops 3225419776 | bytes 14712832 | tf_op jit(solution)/shard_map/nqhk,nkhd->nqhd/dot_general | solution.py:94
  327.7 7.9 %fusion.30 = (f32[32,256]{1,0:T(8,128)S(1)}, f32[32,256]{1,0:T(8,128)S(1)}) fusion(f32[32,256,256]{2,1,0:T(8,128)} %get-tuple-element.47, f32[32,256]{1,0:T(8,128)S(1)} %get-tuple-element.46, f32[32,256]{1,0:T(8,128)S(1)} %get-tuple-element.14, f32[32,256,256]{2,1,0:T(8,128)} %get-tuple-element.49), kind=kLoop, calls=%fused_computation.46 | loop fusion | flops 12566528 | bytes 16908288 | tf_op jit(solution)/shard_map/reduce_sum | solution.py:93
  335.6 17.7 %fusion.24 = f32[32,256,128]{2,1,0:T(8,128)} fusion(f32[32,256,128]{2,1,0:T(8,128)S(1)} %bitcast.488, f32[32,256,256]{2,1,0:T(8,128)} %get-tuple-element.49, f32[32,256]{1,0:T(8,128)S(1)} %get-tuple-element.14), kind=kOutput, calls=%fused_computation.36 | convolution fusion | flops 3225419776 | bytes 16809984 | tf_op jit(solution)/shard_map/nqhk,nkhd->nqhd/dot_general | solution.py:94
  353.4 9.9 %bitcast_reduce_fusion = (f32[2,4096]{1,0:T(2,128)S(1)}, f32[2,256,4096]{2,1,0:T(8,128)S(1)}) fusion(f32[2,256,128]{1,2,0:T(8,128)S(1)} %copy-done.6, f32[2,4096,128]{2,1,0:T(8,128)} %bitcast.82), kind=kOutput, calls=%fused_computation.19 | convolution fusion | flops 3225411584 | bytes 12877824 | tf_op jit(solution)/shard_map/nqhd,nkhd->nqhk/dot_general | solution.py:86
  364.8 17.2 %fusion.27 = f32[32,256,128]{2,1,0:T(8,128)} fusion(f32[32,256,256]{2,1,0:T(8,128)S(1)} %bitcast.463, f32[256,32,128]{2,0,1:T(8,128)} %all-to-all-done.2, f32[32,256]{1,0:T(8,128)S(1)} %get-tuple-element.46), kind=kOutput, calls=%fused_computation.41 | convolution fusion | flops 3225419776 | bytes 16809984 | tf_op jit(solution)/shard_map/nqhk,nkhd->nqhd/dot_general | solution.py:94
  382.0 7.2 %fusion.42 = f32[2,4096,1,128]{1,3,0,2:T(8,128)} fusion(f32[2,256,128]{1,2,0:T(8,128)S(1)} %copy-done.7, f32[2,256,4096]{2,1,0:T(8,128)S(1)} %get-tuple-element.39, f32[2,4096]{1,0:T(2,128)S(1)} %maximum_maximum_fusion), kind=kOutput, calls=%fused_computation.52 | convolution fusion | flops 3225419776 | bytes 12877824 | tf_op jit(solution)/shard_map/nqhk,nkhd->nqhd/dot_general | solution.py:94
  406.1 5.6 copy.74
  417.0 5.8 copy.72
  428.2 5.7 copy.70
  433.9 5.6 copy.68
  450.9 11.1 %fusion.129 = (f32[8192]{0:T(1024)S(1)}, f32[256,8192]{1,0:T(8,128)}) fusion(f32[256,128]{0,1:T(8,128)S(1)} %collective-permute-done, f32[8192,128]{1,0:T(8,128)} %bitcast.99), kind=kOutput, calls=%fused_computation.168 | convolution fusion | flops 3225411584 | bytes 12746752 | tf_op jit(solution)/shard_map/nqhd,nkhd->nqhk/dot_general | solution.py:86
  463.9 11.3 %fusion.128 = (f32[8192]{0:T(1024)S(1)}, f32[256,8192]{1,0:T(8,128)}) fusion(f32[256,128]{0,1:T(8,128)S(1)} %collective-permute-done.2, f32[8192,128]{1,0:T(8,128)} %bitcast.99), kind=kOutput, calls=%fused_computation.167 | convolution fusion | flops 3225411584 | bytes 12746752 | tf_op jit(solution)/shard_map/nqhd,nkhd->nqhk/dot_general | solution.py:86
  484.5 7.8 %fusion.10 = f32[128,8192]{1,0:T(8,128)S(1)} fusion(f32[256,128]{0,1:T(8,128)S(1)} %collective-permute-done.1, f32[256,8192]{1,0:T(8,128)} %get-tuple-element.37, f32[8192]{0:T(1024)S(1)} %get-tuple-element.24), kind=kOutput, calls=%fused_computation.15 | convolution fusion | flops 3223322624 | bytes 12746752 | tf_op jit(solution)/shard_map/nqhk,nkhd->nqhd/dot_general | solution.py:94
  492.4 17.5 %fusion.68 = (f32[8192]{0:T(1024)S(1)}, f32[128,8192]{1,0:T(8,128)}) fusion(f32[128,8192]{1,0:T(8,128)S(1)} %fusion.10, f32[8192,1,128]{0,2,1:T(8,128)} %copy.76, f32[8192,1,128]{0,2,1:T(8,128)} %copy.74, f32[8192,1,128]{0,2,1:T(8,128)} %copy.72, f32[8192,1,128]{0,2,1:T(8,128)} %copy.70, f32[8192,1,128]{0,2,1:T(8,128)} %copy.68, f32[8192,1,128]{0,2,1:T(8,128)} %copy.67, ...), kind=kOutput, calls=%fused_computation.79 | convolution fusion | flops 3242188800 | bytes 42434560 | tf_op jit(solution)/shard_map/nqhk,nkhd->nqhd/dot_general | solution.py:94
  521.3 15.1 %multiply_multiply_fusion = f32[32,256,128]{2,1,0:T(8,128)S(1)} fusion(f32[32,256,128]{2,1,0:T(8,128)} %bitcast.479, f32[32,256,128]{2,1,0:T(8,128)} %bitcast.480, f32[32,256,128]{2,1,0:T(8,128)} %bitcast.466, f32[32,256,128]{2,1,0:T(8,128)} %bitcast.468, f32[32,256,128]{2,1,0:T(8,128)} %bitcast.470, f32[32,256,128]{2,1,0:T(8,128)} %bitcast.472, ...), kind=kLoop, calls=%fused_computation.64 | loop fusion | flops 18874368 | bytes 38076928 | tf_op jit(solution)/shard_map/mul | solution.py:128
  536.3 59.0 %all_to_all.64 = f32[32,256,128]{2,1,0:T(8,128)} all-to-all(f32[32,256,128]{2,1,0:T(8,128)S(1)} %multiply_multiply_fusion), channel_id=1, replica_groups=mesh['ctx'=4,'heads'=32] {'heads'}, dimensions={0} | all-to-all | bytes 8388608 | tf_op jit(solution)/shard_map/all_to_all | solution.py:129
  595.3 5.6 copy.77
  (157 shorter events, 183.3 us)
Async XLA Ops:
  11.2 61.6 %all-to-all-start = ((f32[256,32,128]{2,0,1:T(8,128)}), f32[256,32,128]{2,0,1:T(8,128)}, u32[]{:S(2)}, u32[]{:S(2)}) async-start(f32[256,32,128]{2,0,1:T(8,128)} %copy.28), calls=%async_computation | async-start | bytes 8388608 | tf_op jit(solution)/shard_map/all_to_all | solution.py:112
  72.8 59.2 %all-to-all-start.1 = ((f32[256,32,128]{2,0,1:T(8,128)}), f32[256,32,128]{2,0,1:T(8,128)}, u32[]{:S(2)}, u32[]{:S(2)}) async-start(f32[256,32,128]{2,0,1:T(8,128)} %copy.30), calls=%async_computation.1 | async-start | bytes 8388608 | tf_op jit(solution)/shard_map/all_to_all | solution.py:111
  132.0 100.7 %all-to-all-start.2 = ((f32[256,32,128]{2,0,1:T(8,128)}), f32[256,32,128]{2,0,1:T(8,128)}, u32[]{:S(2)}, u32[]{:S(2)}) async-start(f32[256,32,128]{2,0,1:T(8,128)} %copy.32), calls=%async_computation.2 | async-start | bytes 8388608 | tf_op jit(solution)/shard_map/all_to_all | solution.py:113
  168.8 13.5 %copy-start.8 = (f32[4,2048]{1,0:T(4,128)}, f32[4,2048]{1,0:T(4,128)S(1)}, u32[]{:S(2)}) copy-start(f32[4,2048]{1,0:T(4,128)S(1)} %get-tuple-element.40) | copy-start | bytes 98308
  182.3 44.8 %copy-start.14 = (f32[32,256]{1,0:T(8,128)}, f32[32,256]{1,0:T(8,128)S(1)}, u32[]{:S(2)}) copy-start(f32[32,256]{1,0:T(8,128)S(1)} %reduce_max.113) | copy-start | bytes 98308
  197.0 30.1 %copy-start.16 = (f32[32,256]{1,0:T(8,128)}, f32[32,256]{1,0:T(8,128)S(1)}, u32[]{:S(2)}) copy-start(f32[32,256]{1,0:T(8,128)S(1)} %reduce_max.111) | copy-start | bytes 98308
  202.3 13.7 %copy-start.1 = (f32[16,2,256,128]{3,2,1,0:T(8,128)S(1)}, f32[16,2,256,128]{3,2,1,0:T(8,128)}, u32[]{:S(2)}) copy-start(f32[16,2,256,128]{3,2,1,0:T(8,128)} %rev.26) | copy-start | bytes 12582916
  261.9 183.2 %collective-permute-start = (f32[256,128]{0,1:T(8,128)}, f32[256,128]{0,1:T(8,128)S(1)}, u32[]{:S(2)}, u32[]{:S(2)}) collective-permute-start(f32[256,128]{0,1:T(8,128)} %convolution_bitcast_fusion.5), channel_id=1, source_target_pairs={{0,32},{32,0},{64,96},{96,64},{1,33},{33,1},{65,97},{97,65},{2,34}... | collective-permute-start | bytes 393224 | tf_op jit(solution)/shard_map/ppermute | solution.py:16
  265.5 179.6 %collective-permute-start.1 = (f32[256,128]{0,1:T(8,128)}, f32[256,128]{0,1:T(8,128)S(1)}, u32[]{:S(2)}, u32[]{:S(2)}) collective-permute-start(f32[256,128]{0,1:T(8,128)} %convolution_bitcast_fusion.4), channel_id=1, source_target_pairs={{0,32},{32,0},{64,96},{96,64},{1,33},{33,1},{65,97},{97,65},{2,34}... | collective-permute-start | bytes 393224 | tf_op jit(solution)/shard_map/ppermute | solution.py:16
  270.1 5.5 copy-start.5
  288.8 4.9 copy-start.4
  305.1 1.5 copy-start.10
  306.6 5.0 copy-start.3
  327.7 7.9 %copy-start.2 = (f32[16,2,256,128]{3,2,1,0:T(8,128)S(1)}, f32[16,2,256,128]{3,2,1,0:T(8,128)}, u32[]{:S(2)}) copy-start(f32[16,2,256,128]{3,2,1,0:T(8,128)} %rev.27) | copy-start | bytes 12582916
  335.6 17.7 %copy-start.6 = (f32[2,256,128]{1,2,0:T(8,128)S(1)}, f32[2,256,128]{1,2,0:T(8,128)}, u32[]{:S(2)}) copy-start(f32[2,256,128]{1,2,0:T(8,128)} %reverse.6) | copy-start | bytes 786436
  335.6 29.2 %slice-start = ((s8[8388608]{0:T(1024)(128)(4,1)}), s8[4194304]{0:T(1024)(128)(4,1)S(1)}, s32[]{:S(2)}) async-start(s8[8388608]{0:T(1024)(128)(4,1)} %bitcast.462), calls=%async_computation.4 | async-start | bytes 8388608
  353.3 9.9 %copy-start.19 = (f32[2,4096]{1,0:T(2,128)S(1)}, f32[2,4096]{1,0:T(2,128)}, u32[]{:S(2)}) copy-start(f32[2,4096]{1,0:T(2,128)} %reduce_max.123) | copy-start | bytes 98308
  353.3 9.9 %copy-start.20 = (f32[2,4096]{1,0:T(2,128)S(1)}, f32[2,4096]{1,0:T(2,128)}, u32[]{:S(2)}) copy-start(f32[2,4096]{1,0:T(2,128)} %reduce_max.122) | copy-start | bytes 98308
  353.4 9.9 %copy-start.21 = (f32[2,4096]{1,0:T(2,128)S(1)}, f32[2,4096]{1,0:T(2,128)}, u32[]{:S(2)}) copy-start(f32[2,4096]{1,0:T(2,128)} %reduce_max.121) | copy-start | bytes 98308
  353.4 9.9 %copy-start.22 = (f32[2,4096]{1,0:T(2,128)S(1)}, f32[2,4096]{1,0:T(2,128)}, u32[]{:S(2)}) copy-start(f32[2,4096]{1,0:T(2,128)} %max.382) | copy-start | bytes 98308
  353.4 11.4 %slice-start.1 = ((s8[8388608]{0:T(1024)(128)(4,1)}), s8[4194304]{0:T(1024)(128)(4,1)S(1)}, s32[]{:S(2)}) async-start(s8[8388608]{0:T(1024)(128)(4,1)} %bitcast.462), calls=%async_computation.5 | async-start | bytes 8388608
  364.8 17.2 %copy-start.7 = (f32[2,256,128]{1,2,0:T(8,128)S(1)}, f32[2,256,128]{1,2,0:T(8,128)}, u32[]{:S(2)}) copy-start(f32[2,256,128]{1,2,0:T(8,128)} %reverse.7) | copy-start | bytes 786436
  382.0 7.2 %copy-start.9 = (f32[4,2048]{1,0:T(4,128)S(1)}, f32[4,2048]{1,0:T(4,128)}, u32[]{:S(2)}) copy-start(f32[4,2048]{1,0:T(4,128)} %copy-done.8) | copy-start | bytes 98308
  382.0 7.3 %copy-start.12 = (f32[32,256]{1,0:T(8,128)S(1)}, f32[32,256]{1,0:T(8,128)}, u32[]{:S(2)}) copy-start(f32[32,256]{1,0:T(8,128)} %copy-done.11) | copy-start | bytes 98308
  382.0 7.4 %copy-start.13 = (f32[4,2048]{1,0:T(4,128)S(1)}, f32[4,2048]{1,0:T(4,128)}, u32[]{:S(2)}) copy-start(f32[4,2048]{1,0:T(4,128)} %fusion.38) | copy-start | bytes 98308
  447.9 16.0 %collective-permute-start.2 = (f32[256,128]{0,1:T(8,128)S(1)}, f32[256,128]{0,1:T(8,128)S(1)}, u32[]{:S(2)}, u32[]{:S(2)}) collective-permute-start(f32[256,128]{0,1:T(8,128)S(1)} %convolution_bitcast_fusion.3), channel_id=1, source_target_pairs={{0,64},{64,0},{32,96},{96,32},{1,65},{65,1},{33,97},{97,33},{2,66}... | collective-permute-start | bytes 393224 | tf_op jit(solution)/shard_map/ppermute | solution.py:16
  463.8 28.6 %collective-permute-start.3 = (f32[256,128]{0,1:T(8,128)S(1)}, f32[256,128]{0,1:T(8,128)S(1)}, u32[]{:S(2)}, u32[]{:S(2)}) collective-permute-start(f32[256,128]{0,1:T(8,128)S(1)} %convolution_bitcast_fusion.2), channel_id=1, source_target_pairs={{0,64},{64,0},{32,96},{96,32},{1,65},{65,1},{33,97},{97,33},{2,66}... | collective-permute-start | bytes 393224 | tf_op jit(solution)/shard_map/ppermute | solution.py:16
  492.4 17.6 %copy-start = (f32[128,8192]{1,0:T(8,128)}, f32[128,8192]{1,0:T(8,128)S(1)}, u32[]{:S(2)}) copy-start(f32[128,8192]{1,0:T(8,128)S(1)} %fusion.10) | copy-start | bytes 12582916
  515.5 5.6 copy-start.15
  515.5 5.6 copy-start.17
  515.6 5.6 copy-start.18
  515.6 5.7 copy-start.23
  (1 other events, 0.6 us)
where the time goes:
time: 615 us; the launch traced here: 607 us
  matrix products  242 us (39%)
  local copies, waits for them, and re-layouts  151 us (25%)
  waiting for transfers between devices  71.5 us (12%)
  blocking collectives  59 us (10%)
  other arithmetic  53.8 us (9%)
  starting transfers between devices  29 us (5%)
    dot_general x8, matrix products, absorb(): jnp.einsum('nqhk,nkhd->nqhd', weights.reshape(node_count, per_node, head_...  102 us
    dot_general x8, matrix products, absorb(): jnp.einsum('nqhd,nkhd->nqhk', grouped, key_split, precision=lax.Precision...  92.5 us
    all_to_all x1, blocking collectives, shards(): lax.all_to_all(normed.reshape(query_count, head_count * head_size), 'head...  59 us
    dot_general x12, matrix products, merge_nodes(): jnp.einsum('ij,njw->niw', matrix, paired, precision=lax.Precision.HIGHEST)  47.6 us
    all_to_all x1, waiting for transfers between devices, shards(): lax.all_to_all(keys, 'heads', split_axis=1, concat_axis=0, tiled=True)  40.9 us
    reshape x6, local copies, waits for them, and re-layouts, absorb(): added_values.reshape(query_count, head_count, head_size)  33.9 us
    reduce_sum x7, other arithmetic, absorb(): weight_sum = weight_sum * factor + jnp.sum(weights, axis=-1)  33.8 us
    transpose x6, local copies, waits for them, and re-layouts, absorb(): jnp.einsum('nqhk,nkhd->nqhd', weights.reshape(node_count, per_node, head_...  32.8 us
  transfers between devices with their start and end apart: 7, of which 2 were waited for; matrix products, arithmetic and copies ran while one was open for 57% of the time, Pallas kernels for 0%

commit v1 on v0

v1 whole, which is shorter than its diff:
```python
import functools
import math

import jax
import jax.numpy as jnp
from jax import lax
from jax.experimental import pallas as pl
from jax.experimental.pallas import tpu as pltpu
from jax.sharding import PartitionSpec as P

MESH = pl.DeviceIdType.MESH
F32, BF16 = jnp.float32, jnp.bfloat16
SLOTS = 2
OUT_SLOTS = 2
AHEAD = 3


def tree_levels(ctx, heads):
    z_size = min(4, heads // 2)
    digits = [
        ("heads", 1, 2),
        ("heads", 2, z_size),
        ("heads", 2 * z_size, heads // (2 * z_size)),
        ("ctx", 1, ctx),
    ]
    return [
        (axis, stride, size, bit)
        for axis, stride, size in digits
        for bit in range(size.bit_length() - 1)
    ]


def split(x):
    hi = x.astype(BF16)
    return hi, (x - hi.astype(F32)).astype(BF16)


def halves(x):
    return jnp.concatenate(split(x), axis=1)


def dot(a, b):
    return jnp.dot(a, b, preferred_element_type=F32)


def dot_nt(a, b):
    return lax.dot_general(a, b, (((1,), (1,)), ((), ())), preferred_element_type=F32)


def kernel(
    levels, q, k, v, merge_k, merge_v, gain, out,
    qb, xb, rb, sb, mw, stage, kc, vc, ob, gb,
    load_sem, lend_sem, borrow_sem, send_sem, recv_sem,
    put_sem, give_sem, take_sem, mat_sem, gain_sem, gain_send, gain_recv,
):
    count, rows, width = qb.shape[0], qb.shape[1] // 2, qb.shape[2]
    merges = len(levels) - 1
    here = {axis: lax.axis_index(axis) for axis in ("ctx", "heads")}
    mine = here["heads"]
    core = mine % 2
    args = (k, v, q)
    landing = (xb.at[0], xb.at[1], qb)

    def digit(level):
        axis, stride, size, _ = levels[level]
        return here[axis] // stride % size

    def side(level):
        return digit(level) // 2 ** levels[level][3] % 2

    def partner(level):
        axis, stride, size, bit = levels[level]
        d = digit(level)
        other = size - 1 - d if bit else d + 1 - 2 * (d % 2)
        return {axis: here[axis] + stride * (other - d)}

    partners = [partner(level) for level in range(len(levels))]

    def columns(owner, head):
        return pl.ds(pl.multiple_of((owner * count + head) * width, width), width)

    def leaf(owner):
        return pl.ds(pl.multiple_of(owner * rows, rows), rows)

    def load(i, head):
        return pltpu.make_async_copy(
            args[i].at[:, columns(core, head)],
            landing[i].at[head, leaf(core)],
            load_sem.at[i, head],
        )

    def lend(i, head):
        return pltpu.make_async_remote_copy(
            src_ref=args[i].at[:, columns(1 - core, head)],
            dst_ref=landing[i].at[head, leaf(core)],
            send_sem=lend_sem.at[i, head],
            recv_sem=borrow_sem.at[i, head],
            device_id=partners[0],
            device_id_type=MESH,
        )

    def borrow(i, head):
        return pltpu.make_async_remote_copy(
            src_ref=args[i].at[:, columns(core, head)],
            dst_ref=landing[i].at[head, leaf(1 - core)],
            send_sem=lend_sem.at[i, head],
            recv_sem=borrow_sem.at[i, head],
            device_id=partners[0],
            device_id_type=MESH,
        )

    def pass_on(level, i, head):
        return pltpu.make_async_remote_copy(
            src_ref=sb.at[level, i, head % SLOTS],
            dst_ref=rb.at[level, i, head],
            send_sem=send_sem.at[level, i, head % SLOTS],
            recv_sem=recv_sem.at[level, i, head],
            device_id=partners[level + 1],
            device_id_type=MESH,
        )

    def put(head):
        return pltpu.make_async_copy(
            ob.at[head % OUT_SLOTS, leaf(core)],
            out.at[:, columns(core, head)],
            put_sem.at[head % OUT_SLOTS],
        )

    def give(head):
        return pltpu.make_async_remote_copy(
            src_ref=ob.at[head % OUT_SLOTS, leaf(1 - core)],
            dst_ref=out.at[:, columns(core, head)],
            send_sem=give_sem.at[head % OUT_SLOTS],
            recv_sem=take_sem.at[head],
            device_id=partners[0],
            device_id_type=MESH,
        )

    def take(head):
        return pltpu.make_async_remote_copy(
            src_ref=ob.at[head % OUT_SLOTS, leaf(1 - core)],
            dst_ref=out.at[:, columns(1 - core, head)],
            send_sem=give_sem.at[head % OUT_SLOTS],
            recv_sem=take_sem.at[head],
            device_id=partners[0],
            device_id_type=MESH,
        )

    def matrix(level, i):
        return pltpu.make_async_copy(
            (merge_k, merge_v)[i].at[level], stage.at[2 * level + i], mat_sem.at[level, i]
        )

    gain_levels = [n for n, level in enumerate(levels) if level[0] == "heads"]

    def swap_gain(n, sender):
        span = 2**n
        start = sender // span * span
        return pltpu.make_async_remote_copy(
            src_ref=gb.at[pl.ds(start, span)],
            dst_ref=gb.at[pl.ds(start, span)],
            send_sem=gain_send.at[n],
            recv_sem=gain_recv.at[n],
            device_id=partners[n],
            device_id_type=MESH,
        )

    def gain_step(n):
        if n > 0:
            swap_gain(n - 1, mine).wait_send()
            swap_gain(n - 1, partners[n - 1]["heads"]).wait_recv()
        if n < len(gain_levels):
            swap_gain(n, mine).start()

    own_gain = pltpu.make_async_copy(gain, gb.at[mine], gain_sem)
    own_gain.start()
    for level in range(merges):
        for i in range(2):
            matrix(level, i).start()
    barrier = pltpu.get_barrier_semaphore()
    for other in partners:
        pl.semaphore_signal(barrier, inc=1, device_id=other, device_id_type=MESH)
    pl.semaphore_wait(barrier, len(partners))

    def fetch(i, head):
        lend(i, head).start()
        load(i, head).start()

    for head in range(min(AHEAD, count)):
        fetch(0, head)
        fetch(1, head)
    own_gain.wait()
    for level in range(merges):
        for i in range(2):
            matrix(level, i).wait()
            hi, lo = split(stage[2 * level + i])
            mw[level, i, 0, :rows] = hi[:, :rows]
            mw[level, i, 0, rows:] = lo[:, :rows]
            mw[level, i, 1, :rows] = hi[:, rows:]
            mw[level, i, 1, rows:] = lo[:, rows:]

    def ready(level, i, head):
        if level == 0:
            load(i, head).wait()
            borrow(i, head).wait_recv()
        else:
            pass_on(level - 1, i, head).wait_recv()

        @pl.when(head >= SLOTS)
        def _():
            pass_on(level, i, head - SLOTS).wait_send()

    def merge(level, i, head):
        if level == 0:
            lower, upper = xb[i, head, :rows], xb[i, head, rows:]
            first, second = 0, 1
        else:
            lower, upper = sb[level - 1, i, head % SLOTS], rb[level - 1, i, head]
            first = side(level)
            second = 1 - first
        both = dot(mw[level, i, first], halves(lower)) + dot(mw[level, i, second], halves(upper))
        summed = both[:rows] + both[rows:]
        sb[level, i, head % SLOTS] = summed[:, :width] + summed[:, width:]

    def advance(t, i, guarded):
        if guarded:
            for level in range(merges):
                head = t - level

                @pl.when((head >= 0) & (head < count))
                def _(level=level, head=head):
                    ready(level, i, head)
                    merge(level, i, head)

            for level in range(merges):
                head = t - level

                @pl.when((head >= 0) & (head < count))
                def _(level=level, head=head):
                    pass_on(level, i, head).start()
        else:
            for level in range(merges):
                ready(level, i, t - level)
            for level in range(merges):
                merge(level, i, t - level)
            for level in range(merges):
                pass_on(level, i, t - level).start()

    def attend(head):
        for i in range(2):
            pass_on(merges - 1, i, head).wait_recv()
        for i in range(3):
            lend(i, head).wait_send()
        load(2, head).wait()
        borrow(2, head).wait_recv()
        for cat, i in ((kc, 0), (vc, 1)):
            for n in range(merges + 2):
                block = xb[i, head, n * rows : (n + 1) * rows] if n < 2 else rb[n - 2, i, head]
                cat[n * rows : (n + 1) * rows] = halves(block)

        @pl.when(head >= OUT_SLOTS)
        def _():
            put(head - OUT_SLOTS).wait()
            give(head - OUT_SLOTS).wait_send()

        scale = math.log2(math.e) / math.sqrt(width)
        scale_out = gb[core * count + head]
        hi, lo = kc[:, :width], kc[:, width:]
        keys = jnp.concatenate([hi, hi, lo, lo], axis=1)
        for part in range(2):
            span = slice(part * rows, (part + 1) * rows)
            query = halves(qb[head, span] * scale)
            scores = dot_nt(jnp.concatenate([query, query], axis=1), keys)
            top = jnp.max(scores, axis=1, keepdims=True)
            weights = jnp.exp2(scores - top)
            total = jnp.sum(weights, axis=1, keepdims=True)
            high, low = split(weights)
            both = dot(high, vc[...]) + dot(low, vc[...])
            context = (both[:, :width] + both[:, width:]) / total
            mean_square = jnp.mean(context * context, axis=1, keepdims=True)
            ob[head % OUT_SLOTS, span] = context * lax.rsqrt(mean_square + 1e-06) * scale_out
        put(head).start()
        give(head).start()

    def request(t):
        @pl.when(t + AHEAD < count)
        def _():
            fetch(0, t + AHEAD)
            fetch(1, t + AHEAD)

        @pl.when((t >= AHEAD) & (t - AHEAD < count))
        def _():
            fetch(2, t - AHEAD)

    @pl.loop(0, merges)
    def _(t):
        for n in range(len(gain_levels) + 1):

            @pl.when(t == n)
            def _(n=n):
                gain_step(n)

        request(t)
        advance(t, 0, True)
        advance(t, 1, True)

    @pl.loop(merges, count)
    def _(t):
        request(t)
        advance(t, 0, False)
        advance(t, 1, False)
        attend(t - merges)

    @pl.loop(max(merges, count), count + merges)
    def _(t):
        request(t)
        advance(t, 0, True)
        advance(t, 1, True)
        attend(t - merges)

    for head in range(count - SLOTS, count):
        for level in range(merges):
            for i in range(2):
                pass_on(level, i, head).wait_send()
    for head in range(count - OUT_SLOTS, count):
        put(head).wait()
        give(head).wait_send()

    @pl.loop(0, count)
    def _(head):
        take(head).wait_recv()


def solution(mesh):
    levels = tree_levels(mesh.shape["ctx"], mesh.shape["heads"])
    merges = len(levels) - 1

    def shards(queries, keys, values, merge_keys, merge_values, out_gain):
        rows, columns = queries.shape
        width = out_gain.shape[1]
        heads = columns // width
        count = heads // 2
        gain_steps = sum(level[0] == "heads" for level in levels)
        dma = pltpu.SemaphoreType.DMA
        return pl.pallas_call(
            functools.partial(kernel, levels),
            out_shape=jax.ShapeDtypeStruct((rows, columns), F32),
            in_specs=[pl.BlockSpec(memory_space=pl.ANY)] * 6,
            out_specs=pl.BlockSpec(memory_space=pl.ANY),
            scratch_shapes=[
                pltpu.VMEM((count, 2 * rows, width), F32),
                pltpu.VMEM((2, count, 2 * rows, width), F32),
                pltpu.VMEM((merges, 2, count, rows, width), F32),
                pltpu.VMEM((merges, 2, SLOTS, rows, width), F32),
                pltpu.VMEM((merges, 2, 2, 2 * rows, rows), BF16),
                pltpu.VMEM((2 * merges, rows, 2 * rows), F32),
                pltpu.VMEM(((merges + 2) * rows, 2 * width), BF16),
                pltpu.VMEM(((merges + 2) * rows, 2 * width), BF16),
                pltpu.VMEM((OUT_SLOTS, 2 * rows, width), F32),
                pltpu.VMEM((heads, 1, width), F32),
                dma((3, count)),
                dma((3, count)),
                dma((3, count)),
                dma((merges, 2, SLOTS)),
                dma((merges, 2, count)),
                dma((OUT_SLOTS,)),
                dma((OUT_SLOTS,)),
                dma((count,)),
                dma((merges, 2)),
                dma,
                dma((gain_steps,)),
                dma((gain_steps,)),
            ],
            compiler_params=pltpu.CompilerParams(
                collective_id=0, has_side_effects=True, vmem_limit_bytes=67043328
            ),
            name="multipole",
        )(queries, keys, values, merge_keys, merge_values, out_gain)

    return jax.shard_map(
        shards,
        mesh=mesh,
        in_specs=(
            P(("ctx", "heads"), None),
            P(("ctx", "heads"), None),
            P(("ctx", "heads"), None),
            P(),
            P(),
            P("heads", None),
        ),
        out_specs=P(("ctx", "heads"), None),
        check_vma=False,
    )
```

time: 615 us -> 173 us (0.28); the launches traced: 607 us -> 173 us
  matrix products: 242 us -> 0 us
  Pallas kernels: 0 us -> 168 us
  local copies, waits for them, and re-layouts: 151 us -> 4.65 us
  waiting for transfers between devices: 71.5 us -> 0 us
  blocking collectives: 59 us -> 0 us
  other arithmetic: 53.8 us -> 0 us
  starting transfers between devices: 29 us -> 0 us
    dot_general x28 -> x0, matrix products: 242 us -> none  [the longest x8 102 us: absorb(): jnp.einsum('nqhk,nkhd->nqhd', weights.reshape(node_count, per_node, head_...]
    pallas_call x0 -> x1, Pallas kernels: none -> 168 us  [shards(): pl.pallas_call(functools.partial(kernel, levels), out_shape=jax.ShapeDtyp...]
    all_to_all x3 -> x0, waiting for transfers between devices: 71.5 us -> none  [the longest x1 40.9 us: shards(): lax.all_to_all(keys, 'heads', split_axis=1, concat_axis=0, tiled=True)]
    all_to_all x1 -> x0, blocking collectives: 59 us -> none  [shards(): lax.all_to_all(normed.reshape(query_count, head_count * head_size), 'head...]
    transpose x14 -> x0, local copies, waits for them, and re-layouts: 45 us -> none  [the longest x6 32.8 us: absorb(): jnp.einsum('nqhk,nkhd->nqhd', weights.reshape(node_count, per_node, head_...]
    reshape x6 -> x0, local copies, waits for them, and re-layouts: 33.9 us -> none  [absorb(): added_values.reshape(query_count, head_count, head_size)]
    reduce_sum x7 -> x0, other arithmetic: 33.8 us -> none  [absorb(): weight_sum = weight_sum * factor + jnp.sum(weights, axis=-1)]
    all_to_all x5 -> x0, local copies, waits for them, and re-layouts: 28 us -> none  [the longest x2 11.2 us: shards(): lax.all_to_all(normed.reshape(query_count, head_count * head_size), 'head...]
  transfers between devices with their start and end apart: 7 -> 0, of which waited for: 2 -> 0; matrix products, arithmetic and copies ran while one was open for 57% -> 0% of each run, Pallas kernels for 0% -> 0%
where the time goes in v1:
time: 173 us
  Pallas kernels  168 us (97%)
  local copies, waits for them, and re-layouts  4.65 us (3%)
    pallas_call x1, Pallas kernels, shards(): pl.pallas_call(functools.partial(kernel, levels), out_shape=jax.ShapeDtyp...  168 us
    unnamed x1, local copies, waits for them, and re-layouts  4.65 us

profile of v1, /device:TPU:1, one launch (start us, length us, event | category | flops | bytes accessed | tf_op | source)
XLA Modules:
  0.0 172.9 jit_solution(6210392574539650118)
XLA Ops:
  0.0 168.3 %multipole.1 = f32[256,4096]{1,0:T(8,128)} custom-call(f32[256,4096]{1,0:T(8,128)} %q.1, f32[256,4096]{1,0:T(8,128)} %k.1, f32[256,4096]{1,0:T(8,128)} %v.1, f32[6,256,512]{2,1,0:T(8,128)} %merge_k.1, f32[6,256,512]{2,1,0:T(8,128)} %merge_v.1, f32[1,128]{1,0:T(1,128)} %gain.1), custom_call_target="tpu_custom_call" | custom-call | tf_op jit(solution)/shard_map/multipole/pallas_call | solution.py:345
  168.3 4.7 %copy.8 = f32[256,4096]{1,0:T(8,128)} copy(f32[256,4096]{1,0:T(8,128)} %multipole.1) | data formatting | bytes 8388608

commit v2 on v1

--- a/solution.py
+++ b/solution.py
@@ -13,6 +13,9 @@
 SLOTS = 2
 OUT_SLOTS = 2
 AHEAD = 3
+CHUNK = 16
+STEP = 3
+BEHIND = 2
 
 
 def tree_levels(ctx, heads):
@@ -49,7 +52,7 @@
 
 def kernel(
     levels, q, k, v, merge_k, merge_v, gain, out,
-    qb, xb, rb, sb, mw, stage, kc, vc, ob, gb,
+    qb, xb, rb, sb, mw, stage, kc, vc, wb, tb, ob, gb,
     load_sem, lend_sem, borrow_sem, send_sem, recv_sem,
     put_sem, give_sem, take_sem, mat_sem, gain_sem, gain_send, gain_recv,
 ):
@@ -74,6 +77,9 @@
         other = size - 1 - d if bit else d + 1 - 2 * (d % 2)
         return {axis: here[axis] + stride * (other - d)}
 
+    def sides(level):
+        return side(level) if isinstance(level, int) else 0
+
     partners = [partner(level) for level in range(len(levels))]
 
     def columns(owner, head):
@@ -146,9 +152,14 @@
             device_id_type=MESH,
         )
 
-    def matrix(level, i):
+    def matrix(level, i, which):
+        at = which
+        if not (isinstance(level, int) and level == 0):
+            at = lax.rem(which + sides(level), 2)
         return pltpu.make_async_copy(
-            (merge_k, merge_v)[i].at[level], stage.at[2 * level + i], mat_sem.at[level, i]
+            (merge_k, merge_v)[i].at[level, :, pl.ds(pl.multiple_of(at * rows, rows), rows)],
+            stage.at[2 * level + i, :, pl.ds(which * rows, rows)],
+            mat_sem.at[level, i, which],
         )
 
     gain_levels = [n for n, level in enumerate(levels) if level[0] == "heads"]
@@ -176,7 +187,8 @@
     own_gain.start()
     for level in range(merges):
         for i in range(2):
-            matrix(level, i).start()
+            for which in range(2):
+                matrix(level, i, which).start()
     barrier = pltpu.get_barrier_semaphore()
     for other in partners:
         pl.semaphore_signal(barrier, inc=1, device_id=other, device_id_type=MESH)
@@ -190,14 +202,16 @@
         fetch(0, head)
         fetch(1, head)
     own_gain.wait()
-    for level in range(merges):
+
+    def unpack(level):
         for i in range(2):
-            matrix(level, i).wait()
+            for which in range(2):
+                matrix(level, i, which).wait()
             hi, lo = split(stage[2 * level + i])
-            mw[level, i, 0, :rows] = hi[:, :rows]
-            mw[level, i, 0, rows:] = lo[:, :rows]
-            mw[level, i, 1, :rows] = hi[:, rows:]
-            mw[level, i, 1, rows:] = lo[:, rows:]
+            mw[level, i, :rows] = hi
+            mw[level, i, rows:] = lo
+
+    unpack(0)
 
     def ready(level, i, head):
         if level == 0:
@@ -212,75 +226,102 @@
 
     def merge(level, i, head):
         if level == 0:
-            lower, upper = xb[i, head, :rows], xb[i, head, rows:]
-            first, second = 0, 1
+            first, second = xb[i, head, :rows], xb[i, head, rows:]
         else:
-            lower, upper = sb[level - 1, i, head % SLOTS], rb[level - 1, i, head]
-            first = side(level)
-            second = 1 - first
-        both = dot(mw[level, i, first], halves(lower)) + dot(mw[level, i, second], halves(upper))
+            first, second = sb[level - 1, i, head % SLOTS], rb[level - 1, i, head]
+        pair = jnp.concatenate([halves(first), halves(second)], axis=0)
+        both = dot(mw[level, i], pair)
         summed = both[:rows] + both[rows:]
         sb[level, i, head % SLOTS] = summed[:, :width] + summed[:, width:]
 
-    def advance(t, i, guarded):
+    def when(level, i):
+        return STEP * level + i * BEHIND
+
+    def nodes(t, third):
+        return [
+            (level, i, t - (when(level, i) - third) // 3)
+            for i in range(2)
+            for level in reversed(range(merges))
+            if (when(level, i) - third) % 3 == 0
+        ]
+
+    def advance(t, third, guarded):
+        todo = nodes(t, third)
         if guarded:
-            for level in range(merges):
-                head = t - level
+            for level, i, head in todo:
 
                 @pl.when((head >= 0) & (head < count))
-                def _(level=level, head=head):
+                def _(level=level, i=i, head=head):
                     ready(level, i, head)
                     merge(level, i, head)
 
-            for level in range(merges):
-                head = t - level
+            for level, i, head in todo:
 
                 @pl.when((head >= 0) & (head < count))
-                def _(level=level, head=head):
+                def _(level=level, i=i, head=head):
                     pass_on(level, i, head).start()
         else:
-            for level in range(merges):
-                ready(level, i, t - level)
-            for level in range(merges):
-                merge(level, i, t - level)
-            for level in range(merges):
-                pass_on(level, i, t - level).start()
-
-    def attend(head):
-        for i in range(2):
-            pass_on(merges - 1, i, head).wait_recv()
+            for node in todo:
+                ready(*node)
+            for node in todo:
+                merge(*node)
+            for node in todo:
+                pass_on(*node).start()
+
+    blocks = merges + 2
+    spans = blocks * rows // stage.shape[2]
+
+    def gather(cat, i, head, n):
+        block = xb[i, head, n * rows : (n + 1) * rows] if n < 2 else rb[n - 2, i, head]
+        cat[n * rows : (n + 1) * rows] = halves(block)
+
+    def gathers(cat, i, head):
+        return [functools.partial(gather, cat, i, head, n) for n in range(blocks)]
+
+    def score(head, part):
+        each = stage.shape[2]
+        span = slice(part * rows, (part + 1) * rows)
+        query = halves(qb[head, span] * (math.log2(math.e) / math.sqrt(width)))
+        query = jnp.concatenate([query, query], axis=1)
+        hi, lo = kc[:, :width], kc[:, width:]
+        block = dot_nt(query, jnp.concatenate([hi, hi, lo, lo], axis=1))
+        for n in range(spans):
+            stage[part * spans + n] = block[:, n * each : (n + 1) * each]
+
+    def soften(part, row):
+        scores = jnp.concatenate(
+            [stage[part * spans + n, row : row + CHUNK] for n in range(spans)], axis=1
+        )
+        top = jnp.max(scores, axis=1, keepdims=True)
+        weights = jnp.exp2(scores - top)
+        hi, lo = split(weights)
+        at = part * rows + row
+        tb[at : at + CHUNK] = jnp.sum(weights, axis=1, keepdims=True)
+        wb[at : at + CHUNK] = hi
+        wb[2 * rows + at : 2 * rows + at + CHUNK] = lo
+
+    def softens(part):
+        return [functools.partial(soften, part, row) for row in range(0, rows, CHUNK)]
+
+    def collect(head):
         for i in range(3):
             lend(i, head).wait_send()
-        load(2, head).wait()
-        borrow(2, head).wait_recv()
-        for cat, i in ((kc, 0), (vc, 1)):
-            for n in range(merges + 2):
-                block = xb[i, head, n * rows : (n + 1) * rows] if n < 2 else rb[n - 2, i, head]
-                cat[n * rows : (n + 1) * rows] = halves(block)
 
         @pl.when(head >= OUT_SLOTS)
         def _():
             put(head - OUT_SLOTS).wait()
             give(head - OUT_SLOTS).wait_send()
 
-        scale = math.log2(math.e) / math.sqrt(width)
-        scale_out = gb[core * count + head]
-        hi, lo = kc[:, :width], kc[:, width:]
-        keys = jnp.concatenate([hi, hi, lo, lo], axis=1)
         for part in range(2):
             span = slice(part * rows, (part + 1) * rows)
-            query = halves(qb[head, span] * scale)
-            scores = dot_nt(jnp.concatenate([query, query], axis=1), keys)
-            top = jnp.max(scores, axis=1, keepdims=True)
-            weights = jnp.exp2(scores - top)
-            total = jnp.sum(weights, axis=1, keepdims=True)
-            high, low = split(weights)
-            both = dot(high, vc[...]) + dot(low, vc[...])
-            context = (both[:, :width] + both[:, width:]) / total
+            low = slice((part + 2) * rows, (part + 3) * rows)
+            both = dot(wb[span], vc[...]) + dot(wb[low], vc[...])
+            context = (both[:, :width] + both[:, width:]) / tb[span]
             mean_square = jnp.mean(context * context, axis=1, keepdims=True)
-            ob[head % OUT_SLOTS, span] = context * lax.rsqrt(mean_square + 1e-06) * scale_out
-        put(head).start()
-        give(head).start()
+            normed = context * lax.rsqrt(mean_square + 1e-06)
+            ob[head % OUT_SLOTS, span] = normed * gb[core * count + head]
+
+    lag = -(-max(when(merges - 1, 0) + 3, when(merges - 1, 1) + 1) // 3)
 
     def request(t):
         @pl.when(t + AHEAD < count)
@@ -288,35 +329,60 @@
             fetch(0, t + AHEAD)
             fetch(1, t + AHEAD)
 
-        @pl.when((t >= AHEAD) & (t - AHEAD < count))
+        @pl.when((t >= lag - 2) & (t - lag + 2 < count))
         def _():
-            fetch(2, t - AHEAD)
-
-    @pl.loop(0, merges)
-    def _(t):
-        for n in range(len(gain_levels) + 1):
-
-            @pl.when(t == n)
-            def _(n=n):
-                gain_step(n)
-
-        request(t)
-        advance(t, 0, True)
-        advance(t, 1, True)
-
-    @pl.loop(merges, count)
+            fetch(2, t - lag + 2)
+
+    @pl.loop(0, lag)
     def _(t):
         request(t)
-        advance(t, 0, False)
-        advance(t, 1, False)
-        attend(t - merges)
-
-    @pl.loop(max(merges, count), count + merges)
+        for third in range(3):
+            if third < 2:
+                for n in range(len(gain_levels) + 1):
+                    if n % 2 == third:
+
+                        @pl.when(t == n // 2)
+                        def _(n=n):
+                            gain_step(n)
+
+            advance(t, third, True)
+            for level in range(1, merges):
+                before = when(level, 0) - 2
+                if before % 3 == third:
+
+                    @pl.when(t == before // 3)
+                    def _(level=level):
+                        unpack(level)
+
+    def whole(t, guarded):
+        head = t - lag
+        request(t)
+        advance(t, 0, guarded)
+        pass_on(merges - 1, 0, head).wait_recv()
+        load(2, head).wait()
+        borrow(2, head).wait_recv()
+        for task in gathers(kc, 0, head):
+            task()
+        score(head, 0)
+        advance(t, 1, guarded)
+        score(head, 1)
+        for task in softens(0):
+            task()
+        advance(t, 2, guarded)
+        pass_on(merges - 1, 1, head).wait_recv()
+        for task in gathers(vc, 1, head) + softens(1):
+            task()
+        collect(head)
+        put(head).start()
+        give(head).start()
+
+    @pl.loop(lag, count)
     def _(t):
-        request(t)
-        advance(t, 0, True)
-        advance(t, 1, True)
-        attend(t - merges)
+        whole(t, False)
+
+    @pl.loop(max(lag, count), count + lag)
+    def _(t):
+        whole(t, True)
 
     for head in range(count - SLOTS, count):
         for level in range(merges):
@@ -352,10 +418,12 @@
                 pltpu.VMEM((2, count, 2 * rows, width), F32),
                 pltpu.VMEM((merges, 2, count, rows, width), F32),
                 pltpu.VMEM((merges, 2, SLOTS, rows, width), F32),
-                pltpu.VMEM((merges, 2, 2, 2 * rows, rows), BF16),
+                pltpu.VMEM((merges, 2, 2 * rows, 2 * rows), BF16),
                 pltpu.VMEM((2 * merges, rows, 2 * rows), F32),
                 pltpu.VMEM(((merges + 2) * rows, 2 * width), BF16),
                 pltpu.VMEM(((merges + 2) * rows, 2 * width), BF16),
+                pltpu.VMEM((4 * rows, (merges + 2) * rows), BF16),
+                pltpu.VMEM((2 * rows, 1), F32),
                 pltpu.VMEM((OUT_SLOTS, 2 * rows, width), F32),
                 pltpu.VMEM((heads, 1, width), F32),
                 dma((3, count)),
@@ -366,7 +434,7 @@
                 dma((OUT_SLOTS,)),
                 dma((OUT_SLOTS,)),
                 dma((count,)),
-                dma((merges, 2)),
+                dma((merges, 2, 2)),
                 dma,
                 dma((gain_steps,)),
                 dma((gain_steps,)),

time: 173 us -> 156 us (0.902)
  Pallas kernels: 168 us -> 151 us
    pallas_call x1, Pallas kernels: 168 us -> 151 us  [shards(): pl.pallas_call(functools.partial(kernel, levels), out_shape=jax.ShapeDtyp...]
where the time goes in v2:
time: 156 us; the launch traced here: 155 us
  Pallas kernels  151 us (97%)
  local copies, waits for them, and re-layouts  4.65 us (3%)
    pallas_call x1, Pallas kernels, shards(): pl.pallas_call(functools.partial(kernel, levels), out_shape=jax.ShapeDtyp...  151 us
    unnamed x1, local copies, waits for them, and re-layouts  4.65 us

profile of v2, /device:TPU:1, one launch (start us, length us, event | category | flops | bytes accessed | tf_op | source)
XLA Modules:
  0.0 155.4 jit_solution(17663852266989699821)
XLA Ops:
  0.0 150.7 %multipole.1 = f32[256,4096]{1,0:T(8,128)} custom-call(f32[256,4096]{1,0:T(8,128)} %q.1, f32[256,4096]{1,0:T(8,128)} %k.1, f32[256,4096]{1,0:T(8,128)} %v.1, f32[6,256,512]{2,1,0:T(8,128)} %merge_k.1, f32[6,256,512]{2,1,0:T(8,128)} %merge_v.1, f32[1,128]{1,0:T(1,128)} %gain.1), custom_call_target="tpu_custom_call" | custom-call | tf_op jit(solution)/shard_map/multipole/pallas_call | solution.py:411
  150.7 4.7 %copy.8 = f32[256,4096]{1,0:T(8,128)} copy(f32[256,4096]{1,0:T(8,128)} %multipole.1) | data formatting | bytes 8388608

commit v3 on v2

--- a/solution.py
+++ b/solution.py
@@ -16,6 +16,7 @@
 CHUNK = 16
 STEP = 3
 BEHIND = 2
+GROUPS = 1
 
 
 def tree_levels(ctx, heads):
@@ -185,10 +186,12 @@
 
     own_gain = pltpu.make_async_copy(gain, gb.at[mine], gain_sem)
     own_gain.start()
-    for level in range(merges):
+    def bring(level):
         for i in range(2):
             for which in range(2):
                 matrix(level, i, which).start()
+
+    bring(0)
     barrier = pltpu.get_barrier_semaphore()
     for other in partners:
         pl.semaphore_signal(barrier, inc=1, device_id=other, device_id_type=MESH)
@@ -201,6 +204,9 @@
     for head in range(min(AHEAD, count)):
         fetch(0, head)
         fetch(1, head)
+        if head == 0:
+            for level in range(1, merges):
+                bring(level)
     own_gain.wait()
 
     def unpack(level):
@@ -248,25 +254,35 @@
     def advance(t, third, guarded):
         todo = nodes(t, third)
         if guarded:
-            for level, i, head in todo:
+
+            def send(level, i, head):
+                @pl.when((head >= 0) & (head < count))
+                def _():
+                    pass_on(level, i, head).start()
+
+            earlier = None
+            for level, i, head in reversed(todo):
 
                 @pl.when((head >= 0) & (head < count))
                 def _(level=level, i=i, head=head):
                     ready(level, i, head)
                     merge(level, i, head)
 
-            for level, i, head in todo:
-
-                @pl.when((head >= 0) & (head < count))
-                def _(level=level, i=i, head=head):
-                    pass_on(level, i, head).start()
+                if earlier is not None:
+                    send(*earlier)
+                earlier = (level, i, head)
+            if earlier is not None:
+                send(*earlier)
         else:
-            for node in todo:
-                ready(*node)
-            for node in todo:
-                merge(*node)
-            for node in todo:
-                pass_on(*node).start()
+            size = -(-len(todo) // GROUPS) if todo else 1
+            for at in range(max(0, (len(todo) - 1) // size * size), -1, -size):
+                group = todo[at : at + size]
+                for node in group:
+                    ready(*node)
+                for node in group:
+                    merge(*node)
+                for node in group:
+                    pass_on(*node).start()
 
     blocks = merges + 2
     spans = blocks * rows // stage.shape[2]

time: 156 us -> 152 us (0.974)
  Pallas kernels: 151 us -> 147 us
    pallas_call x1, Pallas kernels: 151 us -> 147 us  [shards(): pl.pallas_call(functools.partial(kernel, levels), out_shape=jax.ShapeDtyp...]
where the time goes in v3:
time: 152 us
  Pallas kernels  147 us (97%)
  local copies, waits for them, and re-layouts  4.65 us (3%)
    pallas_call x1, Pallas kernels, shards(): pl.pallas_call(functools.partial(kernel, levels), out_shape=jax.ShapeDtyp...  147 us
    unnamed x1, local copies, waits for them, and re-layouts  4.65 us

profile of v3, /device:TPU:1, one launch (start us, length us, event | category | flops | bytes accessed | tf_op | source)
XLA Modules:
  0.0 151.7 jit_solution(12818690513562976937)
XLA Ops:
  0.0 147.0 %multipole.1 = f32[256,4096]{1,0:T(8,128)} custom-call(f32[256,4096]{1,0:T(8,128)} %q.1, f32[256,4096]{1,0:T(8,128)} %k.1, f32[256,4096]{1,0:T(8,128)} %v.1, f32[6,256,512]{2,1,0:T(8,128)} %merge_k.1, f32[6,256,512]{2,1,0:T(8,128)} %merge_v.1, f32[1,128]{1,0:T(1,128)} %gain.1), custom_call_target="tpu_custom_call" | custom-call | tf_op jit(solution)/shard_map/multipole/pallas_call | solution.py:427
  147.0 4.7 %copy.8 = f32[256,4096]{1,0:T(8,128)} copy(f32[256,4096]{1,0:T(8,128)} %multipole.1) | data formatting | bytes 8388608
